TPU v7x, 32 devices: a whole 2x2x4 slice. The times are simulated.
32 devices in a mesh: chan: 8 (over z, core), tm: 4 (over y, x).
Axes of the slice: x: 2, y: 2, z: 4, core: 2. Of those that a mesh axis runs over, the one named last changes fastest.
Arguments:
- spectra: bfloat16 [4, 1024, 1024], P('tm', 'chan')
- tile_bin: int32 [32], P('chan'), may hold values from 0 to 7
- owner_bins: int32 [8], replicated, may hold values from 0 to 7, each once
- source_slab: int32 [1], replicated, may hold values from 0 to 255
Outputs:
- stacks: float32 [8, 128, 512], P('chan', 'tm')
Inputs may be any that keep to these rules, and one draw needn't show every extreme that they name: `tile_bin`: a tile of 128 pairs belongs to exactly one offset bin. `owner_bins`: every bin stands once. `source_slab`: the slab's 4 channels lie within one chan index's block.
All inputs are finite; a program needn't handle non-finite values.
Results may differ from a plain program's by a relative error of at most 0.005.
Values may be sent and summed in bfloat16 or wider, within the bound.
A program may use at most 64 MiB of HBM per device.

v0:
```python
import math
import jax
import jax.numpy as jnp
from jax import lax
from jax.sharding import PartitionSpec as P

LAGS = 512
SEG_LEN = 15000
K0 = 60
GROUP = 64
SRC = 4
PAIRS = 128


def shifted(block, axis, distance):
    devices = range(lax.axis_size(axis))
    route = [((i - distance) % len(devices), i) for i in devices]
    return lax.ppermute(block, axis, route)


def whiten_block(raw_block):
    values = raw_block.astype(jnp.float32)
    channels = values.shape[0]
    bands = values.shape[1] // 2
    grouped = values.reshape(channels, 2, bands // GROUP, GROUP)
    power = jnp.mean(grouped[:, 0] * grouped[:, 0] + grouped[:, 1] * grouped[:, 1], axis=-1)
    inverse = 1.0 / jnp.sqrt(power + 1e-06)
    return (grouped * inverse[:, None, :, None]).reshape(channels, 2 * bands).astype(jnp.bfloat16)


def phase_tables(bands, lag_count):
    freq_index = K0 + jnp.arange(bands)
    lag_index = jnp.arange(lag_count) - lag_count // 2
    phase = freq_index[:, None] * lag_index[None, :] % SEG_LEN
    angle = phase.astype(jnp.float32) * (2.0 * math.pi / SEG_LEN)
    return (jnp.cos(angle), jnp.sin(angle))


def modulate(slab_rows, cosines, sines):
    values = slab_rows.astype(jnp.float32)
    bands = cosines.shape[0]
    real_part = values[:, :bands, None]
    imag_part = values[:, bands:, None]
    upper = real_part * cosines[None] + imag_part * sines[None]
    lower = imag_part * cosines[None] - real_part * sines[None]
    return jnp.concatenate([upper, lower], axis=1).astype(jnp.bfloat16)


def normalize(correlation):
    energy = jnp.mean(correlation * correlation, axis=-1, keepdims=True)
    return correlation / jnp.sqrt(energy + 1e-06)


def per_device(spectra, tile_bin, owner_bins, source_slab):
    whitened = whiten_block(spectra[0])
    channels = whitened.shape[0]
    bands = whitened.shape[1] // 2
    cycle_size = lax.axis_size("chan")
    my_index = lax.axis_index("chan")
    slabs_per_block = channels // SRC
    slab_number = source_slab[0]
    root_index = slab_number // slabs_per_block
    own_slab = lax.dynamic_slice_in_dim(whitened, slab_number % slabs_per_block * SRC, SRC, 0)
    initial = jnp.where(my_index == root_index, own_slab, jnp.zeros_like(own_slab))

    def paired_hop(hop_count, state):
        ahead, behind, received = state
        ahead = shifted(ahead, "chan", 1)
        behind = shifted(behind, "chan", -1)
        received = jnp.where((my_index - hop_count) % cycle_size == root_index, ahead, received)
        received = jnp.where((my_index + hop_count) % cycle_size == root_index, behind, received)
        return (ahead, behind, received)

    source_rows = lax.fori_loop(1, cycle_size // 2 + 1, paired_hop, (own_slab, own_slab, initial))[
        2
    ]
    cosines, sines = phase_tables(bands, LAGS)
    modulated = modulate(source_rows, cosines, sines)
    correlation = jnp.einsum("ck,ikl->icl", whitened, modulated, preferred_element_type=jnp.float32)
    traces = normalize(correlation)
    summed = lax.psum(traces, "tm")
    row_count = PAIRS // lax.axis_size("tm")
    own_rows = lax.dynamic_slice_in_dim(summed, lax.axis_index("tm") * row_count, row_count, 1)
    membership = (owner_bins[:, None] == tile_bin[None, :]).astype(jnp.float32)
    stacked = lax.psum_scatter(
        jnp.einsum("rt,tpl->rpl", membership, own_rows, precision=lax.Precision.HIGHEST),
        "chan",
        scatter_dimension=0,
        tiled=True,
    )
    return stacked / lax.axis_size("tm")


def solution(mesh):
    return jax.shard_map(
        per_device,
        mesh=mesh,
        in_specs=(P("tm", "chan", None), P("chan"), P(), P()),
        out_specs=P("chan", "tm", None),
        check_vma=False,
    )
```

profile of v0, /device:TPU:0, one launch (start us, length us, event | category | flops | bytes accessed | tf_op | source)
XLA Modules:
  0.0 135.3 jit_solution(4743199806616281129)
XLA Ops:
  6.5 0.0 all-reduce.2.cloned.1.call-start
  7.3 1.1 copy.14
  8.5 0.1 fusion.11
  8.6 0.1 broadcast_select_fusion
  8.7 0.1 copy.17
  8.9 0.1 copy.15
  9.0 24.5 %while.19 = (s32[]{:T(128)}, bf16[4,1024]{1,0:T(4,128)(2,1)S(1)}, bf16[4,1024]{1,0:T(4,128)(2,1)S(1)}, bf16[4,1024]{1,0:T(4,128)(2,1)S(1)}, s32[]{:T(128)}, /*in...) while((s32[]{:T(128)}, bf16[4,1024]{1,0:T(4,128)(2,1)S(1)}, bf16[4,1024]{1,0:T(4,128)(2,1)S(1)}, ...), condition=%wide.region_2.3_spmd, body=%wide.region_1.2_spmd.sunk | while | flops 8220 | bytes 131515 | solution.py:74
  9.0 4.5 %collective-permute-start.1 = (bf16[4,1024]{1,0:T(4,128)(2,1)S(1)}, bf16[4,1024]{1,0:T(4,128)(2,1)S(1)}, u32[]{:S(2)}, u32[]{:S(2)}) collective-permute-start(bf16[4,1024]{1,0:T(4,128)(2,1)S(1)} %get-tuple-element.246), channel_id=1, source_target_pairs={{4,0},{8,4},{12,8},{16,12},{20,16},{24,20},{28,24},{0,28},{5,1},{9... | collective-permute-start | bytes 24584 | tf_op jit(solution)/shard_map/while/body/eval_jaxpr/ppermute | solution.py:18
  13.6 0.0 collective-permute-start
  13.6 1.4 %collective-permute-done.1 = bf16[4,1024]{1,0:T(4,128)(2,1)S(1)} collective-permute-done((bf16[4,1024]{1,0:T(4,128)(2,1)S(1)}, bf16[4,1024]{1,0:T(4,128)(2,1)S(1)}, u32[]{:S(2)}, u32[]{:S(2)}) %collective-permute-start.1) | collective-permute-done | bytes 8224 | tf_op jit(solution)/shard_map/while/body/eval_jaxpr/ppermute | solution.py:18
  15.0 3.5 %collective-permute-done = bf16[4,1024]{1,0:T(4,128)(2,1)S(1)} collective-permute-done((bf16[4,1024]{1,0:T(4,128)(2,1)S(1)}, bf16[4,1024]{1,0:T(4,128)(2,1)S(1)}, u32[]{:S(2)}, u32[]{:S(2)}) %collective-permute-start) | collective-permute-done | bytes 8224 | tf_op jit(solution)/shard_map/while/body/eval_jaxpr/ppermute | solution.py:18
  18.5 0.1 collective-permute-start.1
  18.6 0.5 collective-permute-start
  19.1 0.9 collective-permute-done.1
  19.9 3.5 %collective-permute-done = bf16[4,1024]{1,0:T(4,128)(2,1)S(1)} collective-permute-done((bf16[4,1024]{1,0:T(4,128)(2,1)S(1)}, bf16[4,1024]{1,0:T(4,128)(2,1)S(1)}, u32[]{:S(2)}, u32[]{:S(2)}) %collective-permute-start) | collective-permute-done | bytes 8224 | tf_op jit(solution)/shard_map/while/body/eval_jaxpr/ppermute | solution.py:18
  23.5 0.1 collective-permute-start.1
  23.6 0.4 collective-permute-start
  24.1 0.9 collective-permute-done.1
  25.0 3.5 %collective-permute-done = bf16[4,1024]{1,0:T(4,128)(2,1)S(1)} collective-permute-done((bf16[4,1024]{1,0:T(4,128)(2,1)S(1)}, bf16[4,1024]{1,0:T(4,128)(2,1)S(1)}, u32[]{:S(2)}, u32[]{:S(2)}) %collective-permute-start) | collective-permute-done | bytes 8224 | tf_op jit(solution)/shard_map/while/body/eval_jaxpr/ppermute | solution.py:18
  28.5 0.1 collective-permute-start.1
  28.6 0.5 collective-permute-start
  29.1 0.9 collective-permute-done.1
  30.0 3.5 %collective-permute-done = bf16[4,1024]{1,0:T(4,128)(2,1)S(1)} collective-permute-done((bf16[4,1024]{1,0:T(4,128)(2,1)S(1)}, bf16[4,1024]{1,0:T(4,128)(2,1)S(1)}, u32[]{:S(2)}, u32[]{:S(2)}) %collective-permute-start) | collective-permute-done | bytes 8224 | tf_op jit(solution)/shard_map/while/body/eval_jaxpr/ppermute | solution.py:18
  33.6 4.3 %fusion.9 = (f32[512,512]{0,1:T(8,128)S(1)}, f32[512,512]{0,1:T(8,128)S(1)}) fusion(s32[512]{0:T(512)S(1)} %get-tuple-element.195, s32[512]{0:T(512)S(1)} %get-tuple-element.196), kind=kLoop, calls=%fused_computation.16 | loop fusion | flops 2359296 | bytes 2101248 | tf_op jit(solution)/shard_map/cos | solution.py:36
  37.9 1.1 add_convert_fusion
  39.0 1.3 multiply_reduce_fusion
  40.3 1.1 divide_bitcast_fusion
  41.4 0.0 copy-start
  41.4 0.0 copy-start.1
  41.4 0.0 all-reduce.2.cloned.1.call-update
  41.4 0.0 reduce-scatter.2.cloned.1.call-start
  41.5 50.9 %all-reduce.2.cloned.1.call-done = f32[4,128,512]{1,2,0:T(8,128)} async-done(((f32[4,128,512]{1,2,0:T(8,128)}), f32[4,128,512]{1,2,0:T(8,128)}) %all-reduce.2.cloned.1.call-update) | async-done | bytes 1048592 | tf_op jit(solution)/shard_map/psum | solution.py:81
  92.3 1.6 %constant_dynamic-slice_fusion = f32[4,32,512]{1,2,0:T(8,128)S(1)} fusion(f32[4,128,512]{1,2,0:T(8,128)} %all-reduce.2.cloned.1.call-done, s32[]{:T(128)S(6)} %select_n.118), kind=kLoop, calls=%fused_computation.36 | loop fusion | bytes 524292 | tf_op jit(solution)/shard_map/dynamic_slice | solution.py:83
  93.9 0.3 copy.19
  94.2 0.0 copy-done
  94.2 0.0 copy-done.1
  94.3 0.5 fusion.15
  94.8 1.1 copy.20
  95.9 0.0 reduce-scatter.2.cloned.1.call-update
  95.9 31.1 %reduce-scatter.2.cloned.1.call-done = f32[1,32,512]{2,1,0:T(8,128)} async-done(((f32[8,32,512]{2,1,0:T(8,128)}), f32[1,32,512]{2,1,0:T(8,128)}) %reduce-scatter.2.cloned.1.call-update) | async-done | bytes 65552 | tf_op jit(solution)/shard_map/reduce_scatter | solution.py:85
  127.0 1.5 %broadcast_multiply_fusion = f32[1,32,512]{2,1,0:T(8,128)} fusion(f32[1,32,512]{2,1,0:T(8,128)} %reduce-scatter.2.cloned.1.call-done), kind=kLoop, calls=%fused_computation.26 | loop fusion | flops 16384 | bytes 131072 | tf_op jit(solution)/shard_map/div | solution.py:91
  (19 shorter events, 0.2 us)
Async XLA Ops:
  6.5 85.8 %all-reduce.2.cloned.1.call-start = ((), (), s32[]{:S(2)}) async-start(), calls=%async_computation.1 | async-start | bytes 2097152 | tf_op jit(solution)/shard_map/psum | solution.py:81
  9.0 5.9 %collective-permute-start.1 = (bf16[4,1024]{1,0:T(4,128)(2,1)S(1)}, bf16[4,1024]{1,0:T(4,128)(2,1)S(1)}, u32[]{:S(2)}, u32[]{:S(2)}) collective-permute-start(bf16[4,1024]{1,0:T(4,128)(2,1)S(1)} %get-tuple-element.246), channel_id=1, source_target_pairs={{4,0},{8,4},{12,8},{16,12},{20,16},{24,20},{28,24},{0,28},{5,1},{9... | collective-permute-start | bytes 24584 | tf_op jit(solution)/shard_map/while/body/eval_jaxpr/ppermute | solution.py:18
  13.6 4.9 %collective-permute-start = (bf16[4,1024]{1,0:T(4,128)(2,1)S(1)}, bf16[4,1024]{1,0:T(4,128)(2,1)S(1)}, u32[]{:S(2)}, u32[]{:S(2)}) collective-permute-start(bf16[4,1024]{1,0:T(4,128)(2,1)S(1)} %get-tuple-element.245), channel_id=1, source_target_pairs={{28,0},{0,4},{4,8},{8,12},{12,16},{16,20},{20,24},{24,28},{29,1},{... | collective-permute-start | bytes 24584 | tf_op jit(solution)/shard_map/while/body/eval_jaxpr/ppermute | solution.py:18
  18.5 1.4 %collective-permute-start.1 = (bf16[4,1024]{1,0:T(4,128)(2,1)S(1)}, bf16[4,1024]{1,0:T(4,128)(2,1)S(1)}, u32[]{:S(2)}, u32[]{:S(2)}) collective-permute-start(bf16[4,1024]{1,0:T(4,128)(2,1)S(1)} %get-tuple-element.246), channel_id=1, source_target_pairs={{4,0},{8,4},{12,8},{16,12},{20,16},{24,20},{28,24},{0,28},{5,1},{9... | collective-permute-start | bytes 24584 | tf_op jit(solution)/shard_map/while/body/eval_jaxpr/ppermute | solution.py:18
  18.6 4.9 %collective-permute-start = (bf16[4,1024]{1,0:T(4,128)(2,1)S(1)}, bf16[4,1024]{1,0:T(4,128)(2,1)S(1)}, u32[]{:S(2)}, u32[]{:S(2)}) collective-permute-start(bf16[4,1024]{1,0:T(4,128)(2,1)S(1)} %get-tuple-element.245), channel_id=1, source_target_pairs={{28,0},{0,4},{4,8},{8,12},{12,16},{16,20},{20,24},{24,28},{29,1},{... | collective-permute-start | bytes 24584 | tf_op jit(solution)/shard_map/while/body/eval_jaxpr/ppermute | solution.py:18
  23.5 1.5 %collective-permute-start.1 = (bf16[4,1024]{1,0:T(4,128)(2,1)S(1)}, bf16[4,1024]{1,0:T(4,128)(2,1)S(1)}, u32[]{:S(2)}, u32[]{:S(2)}) collective-permute-start(bf16[4,1024]{1,0:T(4,128)(2,1)S(1)} %get-tuple-element.246), channel_id=1, source_target_pairs={{4,0},{8,4},{12,8},{16,12},{20,16},{24,20},{28,24},{0,28},{5,1},{9... | collective-permute-start | bytes 24584 | tf_op jit(solution)/shard_map/while/body/eval_jaxpr/ppermute | solution.py:18
  23.6 4.9 %collective-permute-start = (bf16[4,1024]{1,0:T(4,128)(2,1)S(1)}, bf16[4,1024]{1,0:T(4,128)(2,1)S(1)}, u32[]{:S(2)}, u32[]{:S(2)}) collective-permute-start(bf16[4,1024]{1,0:T(4,128)(2,1)S(1)} %get-tuple-element.245), channel_id=1, source_target_pairs={{28,0},{0,4},{4,8},{8,12},{12,16},{16,20},{20,24},{24,28},{29,1},{... | collective-permute-start | bytes 24584 | tf_op jit(solution)/shard_map/while/body/eval_jaxpr/ppermute | solution.py:18
  28.5 1.4 %collective-permute-start.1 = (bf16[4,1024]{1,0:T(4,128)(2,1)S(1)}, bf16[4,1024]{1,0:T(4,128)(2,1)S(1)}, u32[]{:S(2)}, u32[]{:S(2)}) collective-permute-start(bf16[4,1024]{1,0:T(4,128)(2,1)S(1)} %get-tuple-element.246), channel_id=1, source_target_pairs={{4,0},{8,4},{12,8},{16,12},{20,16},{24,20},{28,24},{0,28},{5,1},{9... | collective-permute-start | bytes 24584 | tf_op jit(solution)/shard_map/while/body/eval_jaxpr/ppermute | solution.py:18
  28.6 4.9 %collective-permute-start = (bf16[4,1024]{1,0:T(4,128)(2,1)S(1)}, bf16[4,1024]{1,0:T(4,128)(2,1)S(1)}, u32[]{:S(2)}, u32[]{:S(2)}) collective-permute-start(bf16[4,1024]{1,0:T(4,128)(2,1)S(1)} %get-tuple-element.245), channel_id=1, source_target_pairs={{28,0},{0,4},{4,8},{8,12},{12,16},{16,20},{20,24},{24,28},{29,1},{... | collective-permute-start | bytes 24584 | tf_op jit(solution)/shard_map/while/body/eval_jaxpr/ppermute | solution.py:18
  41.4 52.8 %copy-start = (s32[8]{0:T(128)S(1)}, s32[8]{0:T(128)}, u32[]{:S(2)}) copy-start(s32[8]{0:T(128)} %param.8) | copy-start | bytes 100
  41.4 52.8 %copy-start.1 = (s32[4]{0:T(128)S(1)}, s32[4]{0:T(128)}, u32[]{:S(2)}) copy-start(s32[4]{0:T(128)} %param.7) | copy-start | bytes 52
  41.4 85.5 %reduce-scatter.2.cloned.1.call-start = ((), (), s32[]{:S(2)}) async-start(), calls=%async_computation.2 | async-start | bytes 589824 | tf_op jit(solution)/shard_map/reduce_scatter | solution.py:85
Sparse Core Ops, SparseCore 0:
  41.6 50.7 all-reduce.1
  96.0 30.9 reduce-scatter.1
where the time goes:
time: 136 us; the launch traced here: 135 us
  waiting for transfers between devices  100 us (74%)
  between operations  14.2 us (10%)
  other arithmetic  8.38 us (6%)
  starting transfers between devices  6.27 us (5%)
  local copies, waits for them, and re-layouts  4.45 us (3%)
  matrix products  1.77 us (1%)
    psum x1, waiting for transfers between devices, per_device(): summed = lax.psum(traces, 'tm')  50.9 us
    reduce_scatter x1, waiting for transfers between devices, per_device(): lax.psum_scatter(jnp.einsum('rt,tpl->rpl', membership, own_rows, precisio...  31.1 us
    ppermute x8, waiting for transfers between devices, shifted(): return lax.ppermute(block, axis, route)  18.1 us
    ppermute x8, starting transfers between devices, shifted(): return lax.ppermute(block, axis, route)  6.23 us
    cos x1, other arithmetic, phase_tables(): return (jnp.cos(angle), jnp.sin(angle))  4.29 us
  transfers between devices with their start and end apart: 10, of which 10 were waited for; matrix products, arithmetic and copies ran while one was open for 0% of the time, Pallas kernels for 0%

commit v1 on v0

--- a/solution.py
+++ b/solution.py
@@ -78,7 +78,9 @@
     modulated = modulate(source_rows, cosines, sines)
     correlation = jnp.einsum("ck,ikl->icl", whitened, modulated, preferred_element_type=jnp.float32)
     traces = normalize(correlation)
-    summed = lax.psum(traces, "tm")
+    summed = traces
+    for hop in (1, 2):
+        summed = summed + lax.ppermute(summed, "tm", [(dev, dev ^ hop) for dev in range(4)])
     row_count = PAIRS // lax.axis_size("tm")
     own_rows = lax.dynamic_slice_in_dim(summed, lax.axis_index("tm") * row_count, row_count, 1)
     membership = (owner_bins[:, None] == tile_bin[None, :]).astype(jnp.float32)

time: 136 us -> 125 us (0.919)
  waiting for transfers between devices: 100 us -> 88.7 us
  starting transfers between devices: 6.27 us -> 9.37 us
  local copies, waits for them, and re-layouts: 4.45 us -> 2.57 us
    psum x1 -> x0, waiting for transfers between devices: 50.9 us -> none  [per_device(): summed = lax.psum(traces, 'tm')]
    ppermute x0 -> x2, waiting for transfers between devices: none -> 39.7 us  [per_device(): lax.ppermute(summed, 'tm', [(dev, dev ^ hop) for dev in range(4)])]
    ppermute x0 -> x2, starting transfers between devices: none -> 3.14 us  [per_device(): lax.ppermute(summed, 'tm', [(dev, dev ^ hop) for dev in range(4)])]
    dynamic_slice x2 -> x0, local copies, waits for them, and re-layouts: 1.89 us -> none  [per_device(): lax.dynamic_slice_in_dim(summed, lax.axis_index('tm') * row_count, row_co...]
  transfers between devices with their start and end apart: 10 -> 11, of which waited for: 10 -> 11; matrix products, arithmetic and copies ran while one was open for 0% -> 0% of each run, Pallas kernels for 0% -> 0%
where the time goes in v1:
time: 125 us; the launch traced here: 124 us
  waiting for transfers between devices  88.7 us (71%)
  between operations  14.3 us (11%)
  starting transfers between devices  9.37 us (7%)
  other arithmetic  7.69 us (6%)
  local copies, waits for them, and re-layouts  2.57 us (2%)
  matrix products  1.78 us (1%)
    ppermute x2, waiting for transfers between devices, per_device(): lax.ppermute(summed, 'tm', [(dev, dev ^ hop) for dev in range(4)])  39.7 us
    reduce_scatter x1, waiting for transfers between devices, per_device(): lax.psum_scatter(jnp.einsum('rt,tpl->rpl', membership, own_rows, precisio...  30.9 us
    ppermute x8, waiting for transfers between devices, shifted(): return lax.ppermute(block, axis, route)  18.1 us
    ppermute x8, starting transfers between devices, shifted(): return lax.ppermute(block, axis, route)  6.23 us
    cos x1, other arithmetic, phase_tables(): return (jnp.cos(angle), jnp.sin(angle))  4.28 us
    ppermute x2, starting transfers between devices, per_device(): lax.ppermute(summed, 'tm', [(dev, dev ^ hop) for dev in range(4)])  3.14 us
  transfers between devices with their start and end apart: 11, of which 11 were waited for; matrix products, arithmetic and copies ran while one was open for 0% of the time, Pallas kernels for 0%

profile of v1, /device:TPU:0, one launch (start us, length us, event | category | flops | bytes accessed | tf_op | source)
XLA Modules:
  0.0 124.4 jit_solution(9700316065813235927)
XLA Ops:
  6.5 0.0 reduce-scatter.2.cloned.1.call-start
  7.3 1.1 copy.14
  8.5 0.1 fusion.11
  8.6 0.1 broadcast_select_fusion
  8.7 0.1 copy.17
  8.9 0.1 copy.15
  9.0 24.5 %while.19 = (s32[]{:T(128)}, bf16[4,1024]{1,0:T(4,128)(2,1)S(1)}, bf16[4,1024]{1,0:T(4,128)(2,1)S(1)}, bf16[4,1024]{1,0:T(4,128)(2,1)S(1)}, s32[]{:T(128)}, /*in...) while((s32[]{:T(128)}, bf16[4,1024]{1,0:T(4,128)(2,1)S(1)}, bf16[4,1024]{1,0:T(4,128)(2,1)S(1)}, ...), condition=%wide.region_2.3_spmd, body=%wide.region_1.2_spmd.sunk | while | flops 8220 | bytes 131515 | solution.py:74
  9.0 4.5 %collective-permute-start.1 = (bf16[4,1024]{1,0:T(4,128)(2,1)S(1)}, bf16[4,1024]{1,0:T(4,128)(2,1)S(1)}, u32[]{:S(2)}, u32[]{:S(2)}) collective-permute-start(bf16[4,1024]{1,0:T(4,128)(2,1)S(1)} %get-tuple-element.246), channel_id=1, source_target_pairs={{4,0},{8,4},{12,8},{16,12},{20,16},{24,20},{28,24},{0,28},{5,1},{9... | collective-permute-start | bytes 24584 | tf_op jit(solution)/shard_map/while/body/eval_jaxpr/ppermute | solution.py:18
  13.6 0.0 collective-permute-start
  13.6 1.4 %collective-permute-done.1 = bf16[4,1024]{1,0:T(4,128)(2,1)S(1)} collective-permute-done((bf16[4,1024]{1,0:T(4,128)(2,1)S(1)}, bf16[4,1024]{1,0:T(4,128)(2,1)S(1)}, u32[]{:S(2)}, u32[]{:S(2)}) %collective-permute-start.1) | collective-permute-done | bytes 8224 | tf_op jit(solution)/shard_map/while/body/eval_jaxpr/ppermute | solution.py:18
  15.0 3.5 %collective-permute-done = bf16[4,1024]{1,0:T(4,128)(2,1)S(1)} collective-permute-done((bf16[4,1024]{1,0:T(4,128)(2,1)S(1)}, bf16[4,1024]{1,0:T(4,128)(2,1)S(1)}, u32[]{:S(2)}, u32[]{:S(2)}) %collective-permute-start) | collective-permute-done | bytes 8224 | tf_op jit(solution)/shard_map/while/body/eval_jaxpr/ppermute | solution.py:18
  18.5 0.1 collective-permute-start.1
  18.6 0.5 collective-permute-start
  19.1 0.9 collective-permute-done.1
  19.9 3.5 %collective-permute-done = bf16[4,1024]{1,0:T(4,128)(2,1)S(1)} collective-permute-done((bf16[4,1024]{1,0:T(4,128)(2,1)S(1)}, bf16[4,1024]{1,0:T(4,128)(2,1)S(1)}, u32[]{:S(2)}, u32[]{:S(2)}) %collective-permute-start) | collective-permute-done | bytes 8224 | tf_op jit(solution)/shard_map/while/body/eval_jaxpr/ppermute | solution.py:18
  23.5 0.1 collective-permute-start.1
  23.6 0.4 collective-permute-start
  24.1 0.9 collective-permute-done.1
  25.0 3.5 %collective-permute-done = bf16[4,1024]{1,0:T(4,128)(2,1)S(1)} collective-permute-done((bf16[4,1024]{1,0:T(4,128)(2,1)S(1)}, bf16[4,1024]{1,0:T(4,128)(2,1)S(1)}, u32[]{:S(2)}, u32[]{:S(2)}) %collective-permute-start) | collective-permute-done | bytes 8224 | tf_op jit(solution)/shard_map/while/body/eval_jaxpr/ppermute | solution.py:18
  28.5 0.1 collective-permute-start.1
  28.6 0.5 collective-permute-start
  29.1 0.9 collective-permute-done.1
  30.0 3.5 %collective-permute-done = bf16[4,1024]{1,0:T(4,128)(2,1)S(1)} collective-permute-done((bf16[4,1024]{1,0:T(4,128)(2,1)S(1)}, bf16[4,1024]{1,0:T(4,128)(2,1)S(1)}, u32[]{:S(2)}, u32[]{:S(2)}) %collective-permute-start) | collective-permute-done | bytes 8224 | tf_op jit(solution)/shard_map/while/body/eval_jaxpr/ppermute | solution.py:18
  33.6 4.3 %fusion.9 = (f32[512,512]{1,0:T(8,128)S(1)}, f32[512,512]{1,0:T(8,128)S(1)}) fusion(s32[512]{0:T(512)S(1)} %get-tuple-element.195, s32[512]{0:T(512)S(1)} %get-tuple-element.196), kind=kLoop, calls=%fused_computation.16 | loop fusion | flops 2359296 | bytes 2101248 | tf_op jit(solution)/shard_map/cos | solution.py:36
  37.9 1.2 add_convert_fusion
  39.1 1.2 multiply_reduce_fusion
  40.3 0.1 divide_bitcast_fusion
  40.4 0.0 copy-start
  40.4 0.0 copy-start.1
  40.4 1.6 %collective-permute-start.2 = (f32[4,128,512]{2,1,0:T(8,128)S(1)}, f32[4,128,512]{2,1,0:T(8,128)S(1)}, u32[]{:S(2)}, u32[]{:S(2)}) collective-permute-start(f32[4,128,512]{2,1,0:T(8,128)S(1)} %divide_bitcast_fusion), channel_id=1, source_target_pairs={{0,1},{1,0},{2,3},{3,2},{4,5},{5,4},{6,7},{7,6},{8,9},{9,8},{10,11... | collective-permute-start | bytes 3145736 | tf_op jit(solution)/shard_map/ppermute | solution.py:83
  42.0 20.3 %collective-permute-done.2 = f32[4,128,512]{2,1,0:T(8,128)S(1)} collective-permute-done((f32[4,128,512]{2,1,0:T(8,128)S(1)}, f32[4,128,512]{2,1,0:T(8,128)S(1)}, u32[]{:S(2)}, u32[]{:S(2)}) %collective-permute-start.2) | collective-permute-done | bytes 1048608 | tf_op jit(solution)/shard_map/ppermute | solution.py:83
  62.3 0.2 fusion.23
  62.5 1.6 %collective-permute-start.3 = (f32[4,128,512]{2,1,0:T(8,128)S(1)}, f32[4,128,512]{2,1,0:T(8,128)S(1)}, u32[]{:S(2)}, u32[]{:S(2)}) collective-permute-start(f32[4,128,512]{2,1,0:T(8,128)S(1)} %fusion.23), channel_id=1, source_target_pairs={{0,2},{1,3},{2,0},{3,1},{4,6},{5,7},{6,4},{7,5},{8,10},{9,11},{10,... | collective-permute-start | bytes 3145736 | tf_op jit(solution)/shard_map/ppermute | solution.py:83
  64.1 19.4 %collective-permute-done.3 = f32[4,128,512]{2,1,0:T(8,128)S(1)} collective-permute-done((f32[4,128,512]{2,1,0:T(8,128)S(1)}, f32[4,128,512]{2,1,0:T(8,128)S(1)}, u32[]{:S(2)}, u32[]{:S(2)}) %collective-permute-start.3) | collective-permute-done | bytes 1048608 | tf_op jit(solution)/shard_map/ppermute | solution.py:83
  83.5 0.0 copy-done
  83.5 0.0 copy-done.1
  83.5 0.6 fusion.15
  84.1 1.1 copy.20
  85.2 0.0 reduce-scatter.2.cloned.1.call-update
  85.3 30.9 %reduce-scatter.2.cloned.1.call-done = f32[1,32,512]{2,1,0:T(8,128)} async-done(((f32[8,32,512]{2,1,0:T(8,128)}), f32[1,32,512]{2,1,0:T(8,128)}) %reduce-scatter.2.cloned.1.call-update) | async-done | bytes 65552 | tf_op jit(solution)/shard_map/reduce_scatter | solution.py:87
  116.1 1.5 %broadcast_multiply_fusion = f32[1,32,512]{2,1,0:T(8,128)} fusion(f32[1,32,512]{2,1,0:T(8,128)} %reduce-scatter.2.cloned.1.call-done), kind=kLoop, calls=%fused_computation.29 | loop fusion | flops 16384 | bytes 131072 | tf_op jit(solution)/shard_map/div | solution.py:93
  (20 shorter events, 0.3 us)
Async XLA Ops:
  6.5 109.6 %reduce-scatter.2.cloned.1.call-start = ((), (), s32[]{:S(2)}) async-start(), calls=%async_computation.1 | async-start | bytes 589824 | tf_op jit(solution)/shard_map/reduce_scatter | solution.py:87
  9.0 5.9 %collective-permute-start.1 = (bf16[4,1024]{1,0:T(4,128)(2,1)S(1)}, bf16[4,1024]{1,0:T(4,128)(2,1)S(1)}, u32[]{:S(2)}, u32[]{:S(2)}) collective-permute-start(bf16[4,1024]{1,0:T(4,128)(2,1)S(1)} %get-tuple-element.246), channel_id=1, source_target_pairs={{4,0},{8,4},{12,8},{16,12},{20,16},{24,20},{28,24},{0,28},{5,1},{9... | collective-permute-start | bytes 24584 | tf_op jit(solution)/shard_map/while/body/eval_jaxpr/ppermute | solution.py:18
  13.6 4.9 %collective-permute-start = (bf16[4,1024]{1,0:T(4,128)(2,1)S(1)}, bf16[4,1024]{1,0:T(4,128)(2,1)S(1)}, u32[]{:S(2)}, u32[]{:S(2)}) collective-permute-start(bf16[4,1024]{1,0:T(4,128)(2,1)S(1)} %get-tuple-element.245), channel_id=1, source_target_pairs={{28,0},{0,4},{4,8},{8,12},{12,16},{16,20},{20,24},{24,28},{29,1},{... | collective-permute-start | bytes 24584 | tf_op jit(solution)/shard_map/while/body/eval_jaxpr/ppermute | solution.py:18
  18.5 1.4 %collective-permute-start.1 = (bf16[4,1024]{1,0:T(4,128)(2,1)S(1)}, bf16[4,1024]{1,0:T(4,128)(2,1)S(1)}, u32[]{:S(2)}, u32[]{:S(2)}) collective-permute-start(bf16[4,1024]{1,0:T(4,128)(2,1)S(1)} %get-tuple-element.246), channel_id=1, source_target_pairs={{4,0},{8,4},{12,8},{16,12},{20,16},{24,20},{28,24},{0,28},{5,1},{9... | collective-permute-start | bytes 24584 | tf_op jit(solution)/shard_map/while/body/eval_jaxpr/ppermute | solution.py:18
  18.6 4.9 %collective-permute-start = (bf16[4,1024]{1,0:T(4,128)(2,1)S(1)}, bf16[4,1024]{1,0:T(4,128)(2,1)S(1)}, u32[]{:S(2)}, u32[]{:S(2)}) collective-permute-start(bf16[4,1024]{1,0:T(4,128)(2,1)S(1)} %get-tuple-element.245), channel_id=1, source_target_pairs={{28,0},{0,4},{4,8},{8,12},{12,16},{16,20},{20,24},{24,28},{29,1},{... | collective-permute-start | bytes 24584 | tf_op jit(solution)/shard_map/while/body/eval_jaxpr/ppermute | solution.py:18
  23.5 1.5 %collective-permute-start.1 = (bf16[4,1024]{1,0:T(4,128)(2,1)S(1)}, bf16[4,1024]{1,0:T(4,128)(2,1)S(1)}, u32[]{:S(2)}, u32[]{:S(2)}) collective-permute-start(bf16[4,1024]{1,0:T(4,128)(2,1)S(1)} %get-tuple-element.246), channel_id=1, source_target_pairs={{4,0},{8,4},{12,8},{16,12},{20,16},{24,20},{28,24},{0,28},{5,1},{9... | collective-permute-start | bytes 24584 | tf_op jit(solution)/shard_map/while/body/eval_jaxpr/ppermute | solution.py:18
  23.6 4.9 %collective-permute-start = (bf16[4,1024]{1,0:T(4,128)(2,1)S(1)}, bf16[4,1024]{1,0:T(4,128)(2,1)S(1)}, u32[]{:S(2)}, u32[]{:S(2)}) collective-permute-start(bf16[4,1024]{1,0:T(4,128)(2,1)S(1)} %get-tuple-element.245), channel_id=1, source_target_pairs={{28,0},{0,4},{4,8},{8,12},{12,16},{16,20},{20,24},{24,28},{29,1},{... | collective-permute-start | bytes 24584 | tf_op jit(solution)/shard_map/while/body/eval_jaxpr/ppermute | solution.py:18
  28.5 1.4 %collective-permute-start.1 = (bf16[4,1024]{1,0:T(4,128)(2,1)S(1)}, bf16[4,1024]{1,0:T(4,128)(2,1)S(1)}, u32[]{:S(2)}, u32[]{:S(2)}) collective-permute-start(bf16[4,1024]{1,0:T(4,128)(2,1)S(1)} %get-tuple-element.246), channel_id=1, source_target_pairs={{4,0},{8,4},{12,8},{16,12},{20,16},{24,20},{28,24},{0,28},{5,1},{9... | collective-permute-start | bytes 24584 | tf_op jit(solution)/shard_map/while/body/eval_jaxpr/ppermute | solution.py:18
  28.6 4.9 %collective-permute-start = (bf16[4,1024]{1,0:T(4,128)(2,1)S(1)}, bf16[4,1024]{1,0:T(4,128)(2,1)S(1)}, u32[]{:S(2)}, u32[]{:S(2)}) collective-permute-start(bf16[4,1024]{1,0:T(4,128)(2,1)S(1)} %get-tuple-element.245), channel_id=1, source_target_pairs={{28,0},{0,4},{4,8},{8,12},{12,16},{16,20},{20,24},{24,28},{29,1},{... | collective-permute-start | bytes 24584 | tf_op jit(solution)/shard_map/while/body/eval_jaxpr/ppermute | solution.py:18
  40.4 43.1 %copy-start = (s32[8]{0:T(128)S(1)}, s32[8]{0:T(128)}, u32[]{:S(2)}) copy-start(s32[8]{0:T(128)} %param.8) | copy-start | bytes 100
  40.4 43.1 %copy-start.1 = (s32[4]{0:T(128)S(1)}, s32[4]{0:T(128)}, u32[]{:S(2)}) copy-start(s32[4]{0:T(128)} %param.7) | copy-start | bytes 52
  40.4 21.9 %collective-permute-start.2 = (f32[4,128,512]{2,1,0:T(8,128)S(1)}, f32[4,128,512]{2,1,0:T(8,128)S(1)}, u32[]{:S(2)}, u32[]{:S(2)}) collective-permute-start(f32[4,128,512]{2,1,0:T(8,128)S(1)} %divide_bitcast_fusion), channel_id=1, source_target_pairs={{0,1},{1,0},{2,3},{3,2},{4,5},{5,4},{6,7},{7,6},{8,9},{9,8},{10,11... | collective-permute-start | bytes 3145736 | tf_op jit(solution)/shard_map/ppermute | solution.py:83
  62.5 20.9 %collective-permute-start.3 = (f32[4,128,512]{2,1,0:T(8,128)S(1)}, f32[4,128,512]{2,1,0:T(8,128)S(1)}, u32[]{:S(2)}, u32[]{:S(2)}) collective-permute-start(f32[4,128,512]{2,1,0:T(8,128)S(1)} %fusion.23), channel_id=1, source_target_pairs={{0,2},{1,3},{2,0},{3,1},{4,6},{5,7},{6,4},{7,5},{8,10},{9,11},{10,... | collective-permute-start | bytes 3145736 | tf_op jit(solution)/shard_map/ppermute | solution.py:83
Sparse Core Ops, SparseCore 0:
  85.4 30.6 reduce-scatter.1
